TPU v7x, 256 devices: a whole 4x4x8 slice. The times are simulated.
256 devices in a mesh: smp: 32 (over x_lo, z, core), par: 8 (over x_hi, y).
Axes of the slice: x: 4 (x_hi: 2, x_lo: 2; x = x_hi * 2 + x_lo), y: 4, z: 8, core: 2. Of those that a mesh axis runs over, the one named last changes fastest.
Arguments:
- log_derivs: float32 [8192, 8192], P('smp', 'par'), may hold values from -40 to 40, as said below
- coefficients: float32 [8192], P('smp'), may hold values from -6 to 6
Outputs:
- gram: float32 [8192, 8192], P('smp', 'par')
- update: float32 [8192], P(('par', 'smp'))
Inputs may be any that keep to these rules, and one draw needn't show every extreme that they name: `log_derivs`: finite real values.
All inputs are finite; a program needn't handle non-finite values.
Results may differ from a plain program's by a relative error of at most 0.00014.
Values sent between devices are 32-bit elements; how exact they have to be, the bound alone decides.
A program may use at most 128 MiB of HBM per device.

v0:
```python
import jax
import jax.numpy as jnp
from jax import lax
from jax.sharding import PartitionSpec as P


def row_products(left_rows, right_rows):
    return lax.dot_general(
        left_rows,
        right_rows,
        (((1,), (1,)), ((), ())),
        precision=lax.Precision.HIGHEST,
        preferred_element_type=jnp.float32,
    )


def local(log_derivs, coefficients):
    samples = log_derivs.shape[0] * lax.axis_size("smp")
    column_total = lax.psum(jnp.sum(log_derivs, axis=0), "smp")
    centred = (log_derivs - column_total[None, :] / samples) / jnp.sqrt(jnp.float32(samples))
    partial_gram = row_products(centred, lax.all_gather(centred, "smp", axis=0, tiled=True))
    gram = lax.psum_scatter(partial_gram, "par", scatter_dimension=1, tiled=True)
    update_term = lax.dot_general(
        coefficients,
        centred,
        (((0,), (0,)), ((), ())),
        precision=lax.Precision.HIGHEST,
        preferred_element_type=jnp.float32,
    )
    update = lax.psum_scatter(update_term, "smp", scatter_dimension=0, tiled=True)
    return (gram, update)


def solution(mesh):
    placed = (P("smp", "par"), P("smp"))
    return jax.shard_map(
        local,
        mesh=mesh,
        in_specs=placed,
        out_specs=(P("smp", "par"), P(("par", "smp"))),
        check_vma=False,
    )
```

profile of v0, /device:TPU:1, one launch (start us, length us, event | category | flops | bytes accessed | tf_op | source)
XLA Modules:
  0.0 410.7 jit_solution(7156183414748305137)
XLA Ops:
  7.2 0.0 copy-start
  7.2 0.0 all-gather.2.cloned.1.call-start
  7.2 1.3 reduce_sum.9
  8.5 56.9 %psum.7 = f32[1024]{0:T(1024)S(1)} all-reduce(f32[1024]{0:T(1024)S(1)} %reduce_sum.9), channel_id=1, replica_groups=mesh['smp'=32,'par'=8] {'smp'}, use_global_device_ids=true, to_apply=%region_1.0 | all-reduce | flops 1024 | bytes 8192 | tf_op jit(solution)/shard_map/psum | solution.py:19
  65.4 2.4 subtract_multiply_fusion
  67.8 0.0 all-gather.2.cloned.1.call-update
  67.8 0.0 copy-start.2
  67.8 0.0 copy-start.1
  67.9 0.0 reduce-scatter.2.cloned.1.call-start
  67.9 183.8 %all-gather.2.cloned.1.call-done = f32[8192,1024]{1,0:T(8,128)} async-done(((f32[256,1024]{1,0:T(8,128)}), f32[8192,1024]{1,0:T(8,128)}) %all-gather.2.cloned.1.call-update) | async-done | bytes 33554448 | tf_op jit(solution)/shard_map/all_gather | solution.py:21
  251.7 33.2 %fusion = f32[256,8192]{1,0:T(8,128)} fusion(f32[256,1024]{1,0:T(8,128)} %subtract_multiply_fusion, f32[8192,1024]{1,0:T(8,128)} %all-gather.2.cloned.1.call-done), kind=kOutput, calls=%fused_computation.2 | convolution fusion | flops 25769803776 | bytes 42991616 | tf_op jit(solution)/shard_map/dot_general | solution.py:8
  284.9 0.0 reduce-scatter.2.cloned.1.call-update
  285.0 0.0 copy-done.2
  285.0 0.6 dynamic-slice
  286.2 0.0 copy-done
  286.2 0.0 copy-done.1
  286.2 0.6 fusion.1
  286.9 53.7 %all-reduce = f32[1024]{0:T(1024)S(1)} all-reduce(f32[1024]{0:T(1024)S(1)} %bitcast.8), channel_id=3, replica_groups=mesh['smp'=32,'par'=8] {'smp'}, use_global_device_ids=true, to_apply=%region_3.0.clone | all-reduce | flops 1024 | bytes 8192
  340.6 0.6 dynamic-slice.1
  341.2 62.6 %reduce-scatter.2.cloned.1.call-done = f32[256,1024]{1,0:T(8,128)} async-done(((f32[256,8192]{1,0:T(8,128)}), f32[256,1024]{1,0:T(8,128)}) %reduce-scatter.2.cloned.1.call-update) | async-done | bytes 1048592 | tf_op jit(solution)/shard_map/reduce_scatter | solution.py:22
  (1 shorter events, 0.0 us)
Async XLA Ops:
  7.2 279.1 %copy-start = (f32[256]{0:T(256)S(1)}, f32[256]{0:T(256)}, u32[]{:S(2)}) copy-start(f32[256]{0:T(256)} %param.3) | copy-start | bytes 3076
  7.2 244.5 %all-gather.2.cloned.1.call-start = ((), (), s32[]{:S(2)}) async-start(), calls=%async_computation.1 | async-start | bytes 34603008 | tf_op jit(solution)/shard_map/all_gather | solution.py:21
  67.8 217.1 %copy-start.2 = (u32[256]{0:T(256)S(1)}, u32[256]{0:T(256)}, u32[]{:S(2)}) copy-start(u32[256]{0:T(256)} %constant.10) | copy-start | bytes 3076
  67.8 218.4 %copy-start.1 = (f32[256,1024]{1,0:T(8,128)S(1)}, f32[256,1024]{1,0:T(8,128)}, u32[]{:S(2)}) copy-start(f32[256,1024]{1,0:T(8,128)} %subtract_multiply_fusion) | copy-start | bytes 3145732
  67.9 336.0 %reduce-scatter.2.cloned.1.call-start = ((), (), s32[]{:S(2)}) async-start(), calls=%async_computation.2 | async-start | bytes 9437184 | tf_op jit(solution)/shard_map/reduce_scatter | solution.py:22
Sparse Core Ops, SparseCore 0:
  67.9 183.7 all-gather.1
  285.1 118.6 reduce-scatter.1
where the time goes:
time: 411 us
  waiting for transfers between devices  246 us (60%)
  blocking collectives  111 us (27%)
  matrix products  33.9 us (8%)
  between operations  14.7 us (4%)
    all_gather x1, waiting for transfers between devices, local(): lax.all_gather(centred, 'smp', axis=0, tiled=True)  184 us
    reduce_scatter x1, waiting for transfers between devices, local(): lax.psum_scatter(partial_gram, 'par', scatter_dimension=1, tiled=True)  62.6 us
    psum x1, blocking collectives, local(): column_total = lax.psum(jnp.sum(log_derivs, axis=0), 'smp')  56.9 us
    unnamed x1, blocking collectives  53.7 us
    dot_general x1, matrix products, row_products(): lax.dot_general(left_rows, right_rows, (((1,), (1,)), ((), ())), precisio...  33.2 us
  transfers between devices with their start and end apart: 2, of which 2 were waited for; matrix products, arithmetic and copies ran while one was open for 0% of the time, Pallas kernels for 0%

commit v1 on v0

--- a/solution.py
+++ b/solution.py
@@ -15,8 +15,12 @@
 
 
 def local(log_derivs, coefficients):
+
+    def prepare_leaf(v0, mesh_name):
+        return jnp.sum(lax.all_gather(v0, mesh_name), axis=0)
+
     samples = log_derivs.shape[0] * lax.axis_size("smp")
-    column_total = lax.psum(jnp.sum(log_derivs, axis=0), "smp")
+    column_total = prepare_leaf(jnp.sum(log_derivs, axis=0), "smp")
     centred = (log_derivs - column_total[None, :] / samples) / jnp.sqrt(jnp.float32(samples))
     partial_gram = row_products(centred, lax.all_gather(centred, "smp", axis=0, tiled=True))
     gram = lax.psum_scatter(partial_gram, "par", scatter_dimension=1, tiled=True)

time: 411 us -> 389 us (0.946)
  blocking collectives: 111 us -> 92.5 us
    psum x1 -> x0, blocking collectives: 56.9 us -> none  [local(): column_total = lax.psum(jnp.sum(log_derivs, axis=0), 'smp')]
    all_gather x0 -> x1, blocking collectives: none -> 38.8 us  [prepare_leaf(): return jnp.sum(lax.all_gather(v0, mesh_name), axis=0)]
where the time goes in v1:
time: 389 us
  waiting for transfers between devices  243 us (62%)
  blocking collectives  92.5 us (24%)
  matrix products  33.9 us (9%)
  between operations  14.8 us (4%)
    all_gather x1, waiting for transfers between devices, local(): lax.all_gather(centred, 'smp', axis=0, tiled=True)  180 us
    reduce_scatter x1, waiting for transfers between devices, local(): lax.psum_scatter(partial_gram, 'par', scatter_dimension=1, tiled=True)  62.4 us
    unnamed x1, blocking collectives  53.7 us
    all_gather x1, blocking collectives, prepare_leaf(): return jnp.sum(lax.all_gather(v0, mesh_name), axis=0)  38.8 us
    dot_general x1, matrix products, row_products(): lax.dot_general(left_rows, right_rows, (((1,), (1,)), ((), ())), precisio...  33.2 us
  transfers between devices with their start and end apart: 2, of which 2 were waited for; matrix products, arithmetic and copies ran while one was open for 0% of the time, Pallas kernels for 0%

profile of v1, /device:TPU:1, one launch (start us, length us, event | category | flops | bytes accessed | tf_op | source)
XLA Modules:
  0.0 388.8 jit_solution(12788124747997990614)
XLA Ops:
  7.2 0.0 copy-start
  7.2 0.0 all-gather.3.cloned.1.call-start
  7.2 1.3 reduce_sum.18
  8.5 38.8 %all-gather = f32[32768]{0:T(1024)S(1)} all-gather(f32[1024]{0:T(1024)S(1)} %reduce_sum.18), channel_id=2, replica_groups=mesh['smp'=32,'par'=8] {'smp'}, dimensions={0}, use_global_device_ids=true | all-gather | bytes 135168 | tf_op jit(solution)/shard_map/all_gather | solution.py:20
  47.4 2.4 subtract_multiply_fusion
  49.8 0.0 all-gather.3.cloned.1.call-update
  49.8 0.0 copy-start.2
  49.8 0.0 copy-start.1
  49.8 0.0 reduce-scatter.2.cloned.1.call-start
  49.9 180.2 %all-gather.3.cloned.1.call-done = f32[8192,1024]{1,0:T(8,128)} async-done(((f32[256,1024]{1,0:T(8,128)}), f32[8192,1024]{1,0:T(8,128)}) %all-gather.3.cloned.1.call-update) | async-done | bytes 33554448 | tf_op jit(solution)/shard_map/all_gather | solution.py:25
  230.1 33.2 %fusion = f32[256,8192]{1,0:T(8,128)} fusion(f32[256,1024]{1,0:T(8,128)} %subtract_multiply_fusion, f32[8192,1024]{1,0:T(8,128)} %all-gather.3.cloned.1.call-done), kind=kOutput, calls=%fused_computation.2 | convolution fusion | flops 25769803776 | bytes 42991616 | tf_op jit(solution)/shard_map/dot_general | solution.py:8
  263.3 0.0 reduce-scatter.2.cloned.1.call-update
  263.3 0.0 copy-done.2
  263.3 0.6 dynamic-slice
  264.6 0.0 copy-done
  264.6 0.0 copy-done.1
  264.6 0.6 fusion.1
  265.2 53.7 %all-reduce = f32[1024]{0:T(1024)S(1)} all-reduce(f32[1024]{0:T(1024)S(1)} %bitcast.8), channel_id=4, replica_groups=mesh['smp'=32,'par'=8] {'smp'}, use_global_device_ids=true, to_apply=%region_3.0.clone | all-reduce | flops 1024 | bytes 8192
  318.9 0.6 dynamic-slice.1
  319.5 62.4 %reduce-scatter.2.cloned.1.call-done = f32[256,1024]{1,0:T(8,128)} async-done(((f32[256,8192]{1,0:T(8,128)}), f32[256,1024]{1,0:T(8,128)}) %reduce-scatter.2.cloned.1.call-update) | async-done | bytes 1048592 | tf_op jit(solution)/shard_map/reduce_scatter | solution.py:26
  (3 shorter events, 0.1 us)
Async XLA Ops:
  7.2 257.4 %copy-start = (f32[256]{0:T(256)S(1)}, f32[256]{0:T(256)}, u32[]{:S(2)}) copy-start(f32[256]{0:T(256)} %param.3) | copy-start | bytes 3076
  7.2 222.9 %all-gather.3.cloned.1.call-start = ((), (), s32[]{:S(2)}) async-start(), calls=%async_computation.1 | async-start | bytes 34603008 | tf_op jit(solution)/shard_map/all_gather | solution.py:25
  49.8 213.5 %copy-start.2 = (u32[256]{0:T(256)S(1)}, u32[256]{0:T(256)}, u32[]{:S(2)}) copy-start(u32[256]{0:T(256)} %constant.10) | copy-start | bytes 3076
  49.8 214.7 %copy-start.1 = (f32[256,1024]{1,0:T(8,128)S(1)}, f32[256,1024]{1,0:T(8,128)}, u32[]{:S(2)}) copy-start(f32[256,1024]{1,0:T(8,128)} %subtract_multiply_fusion) | copy-start | bytes 3145732
  49.8 332.1 %reduce-scatter.2.cloned.1.call-start = ((), (), s32[]{:S(2)}) async-start(), calls=%async_computation.2 | async-start | bytes 9437184 | tf_op jit(solution)/shard_map/reduce_scatter | solution.py:26
Sparse Core Ops, SparseCore 0:
  49.9 180.0 all-gather.2
  263.4 118.4 reduce-scatter.1

commit v2 on v0

--- a/solution.py
+++ b/solution.py
@@ -18,7 +18,13 @@
     samples = log_derivs.shape[0] * lax.axis_size("smp")
     column_total = lax.psum(jnp.sum(log_derivs, axis=0), "smp")
     centred = (log_derivs - column_total[None, :] / samples) / jnp.sqrt(jnp.float32(samples))
-    partial_gram = row_products(centred, lax.all_gather(centred, "smp", axis=0, tiled=True))
+    partial_gram = row_products(
+        centred,
+        jnp.concatenate(
+            lax.all_to_all(jnp.stack([centred for _ in range(lax.axis_size("smp"))]), "smp", 0, 0),
+            0,
+        ),
+    )
     gram = lax.psum_scatter(partial_gram, "par", scatter_dimension=1, tiled=True)
     update_term = lax.dot_general(
         coefficients,

time: 411 us -> 960 us (2.34)
  blocking collectives: 111 us -> 843 us
  waiting for transfers between devices: 246 us -> 60.1 us
    all_to_all x0 -> x1, blocking collectives: none -> 731 us  [local(): lax.all_to_all(jnp.stack([centred for _ in range(lax.axis_size('smp'))]),...]
    all_gather x1 -> x0, waiting for transfers between devices: 184 us -> none  [local(): lax.all_gather(centred, 'smp', axis=0, tiled=True)]
  transfers between devices with their start and end apart: 2 -> 1, of which waited for: 2 -> 1; matrix products, arithmetic and copies ran while one was open for 0% -> 0% of each run, Pallas kernels for 0% -> 0%
where the time goes in v2:
time: 960 us
  blocking collectives  843 us (88%)
  waiting for transfers between devices  60.1 us (6%)
  matrix products  33.6 us (4%)
  between operations  14.7 us (2%)
    all_to_all x1, blocking collectives, local(): lax.all_to_all(jnp.stack([centred for _ in range(lax.axis_size('smp'))]),...  731 us
    reduce_scatter x1, waiting for transfers between devices, local(): lax.psum_scatter(partial_gram, 'par', scatter_dimension=1, tiled=True)  60.1 us
    psum x1, blocking collectives, local(): column_total = lax.psum(jnp.sum(log_derivs, axis=0), 'smp')  56.9 us
    unnamed x1, blocking collectives  55.6 us
    dot_general x1, matrix products, row_products(): lax.dot_general(left_rows, right_rows, (((1,), (1,)), ((), ())), precisio...  33 us
  transfers between devices with their start and end apart: 1, of which 1 were waited for; matrix products, arithmetic and copies ran while one was open for 0% of the time, Pallas kernels for 0%

profile of v2, /device:TPU:1, one launch (start us, length us, event | category | flops | bytes accessed | tf_op | source)
XLA Modules:
  0.0 959.6 jit_solution(8777809159813791825)
XLA Ops:
  7.2 0.0 copy-start
  7.2 0.0 reduce-scatter.2.cloned.1.call-start
  7.2 1.3 reduce_sum.9
  8.5 56.9 %psum.7 = f32[1024]{0:T(1024)S(1)} all-reduce(f32[1024]{0:T(1024)S(1)} %reduce_sum.9), channel_id=1, replica_groups=mesh['smp'=32,'par'=8] {'smp'}, use_global_device_ids=true, to_apply=%region_1.0 | all-reduce | flops 1024 | bytes 8192 | tf_op jit(solution)/shard_map/psum | solution.py:19
  65.4 1.3 subtract_multiply_fusion
  66.8 4.3 stack.2
  71.0 730.6 %all_to_all.5 = f32[32,256,1024]{2,1,0:T(8,128)} all-to-all(f32[32,256,1024]{2,1,0:T(8,128)S(1)} %stack.2), channel_id=1, replica_groups=mesh['smp'=32,'par'=8] {'smp'}, dimensions={0} | all-to-all | bytes 67108864 | tf_op jit(solution)/shard_map/all_to_all | solution.py:24
  801.6 0.0 copy-start.1
  801.7 33.0 %fusion = f32[256,8192]{1,0:T(8,128)} fusion(f32[256,1024]{1,0:T(8,128)S(1)} %subtract_multiply_fusion, f32[8192,1024]{1,0:T(8,128)} %bitcast.9), kind=kOutput, calls=%fused_computation.2 | convolution fusion | flops 25769803776 | bytes 42991616 | tf_op jit(solution)/shard_map/dot_general | solution.py:8
  834.6 0.0 reduce-scatter.2.cloned.1.call-update
  834.7 0.0 copy-done.1
  834.7 0.6 dynamic-slice
  835.9 0.0 copy-done
  835.9 0.6 fusion.1
  836.6 55.6 %all-reduce = f32[1024]{0:T(1024)S(1)} all-reduce(f32[1024]{0:T(1024)S(1)} %bitcast.10), channel_id=3, replica_groups=mesh['smp'=32,'par'=8] {'smp'}, use_global_device_ids=true, to_apply=%region_3.0.clone | all-reduce | flops 1024 | bytes 8192
  892.1 0.6 dynamic-slice.1
  892.7 60.1 %reduce-scatter.2.cloned.1.call-done = f32[256,1024]{1,0:T(8,128)} async-done(((f32[256,8192]{1,0:T(8,128)}), f32[256,1024]{1,0:T(8,128)}) %reduce-scatter.2.cloned.1.call-update) | async-done | bytes 1048592 | tf_op jit(solution)/shard_map/reduce_scatter | solution.py:28
  (1 shorter events, 0.0 us)
Async XLA Ops:
  7.2 828.8 %copy-start = (f32[256]{0:T(256)S(1)}, f32[256]{0:T(256)}, u32[]{:S(2)}) copy-start(f32[256]{0:T(256)} %param.3) | copy-start | bytes 3076
  7.2 945.6 %reduce-scatter.2.cloned.1.call-start = ((), (), s32[]{:S(2)}) async-start(), calls=%async_computation.2 | async-start | bytes 9437184 | tf_op jit(solution)/shard_map/reduce_scatter | solution.py:28
  801.6 33.0 %copy-start.1 = (u32[256]{0:T(256)S(1)}, u32[256]{0:T(256)}, u32[]{:S(2)}) copy-start(u32[256]{0:T(256)} %constant.10) | copy-start | bytes 3076
Sparse Core Ops, SparseCore 0:
  834.8 117.9 reduce-scatter.1
